TPU v7x, 32 devices: a whole 2x2x4 slice. The times are simulated.
32 devices in a mesh: tx: 2 (over core), ty: 4 (over y, x), lz: 4 (over z).
Axes of the slice: x: 2, y: 2, z: 4, core: 2. Of those that a mesh axis runs over, the one named last changes fastest.
Arguments:
- test_field: bfloat16 [64, 6, 48, 512], P('tx', None, 'lz', 'ty'), may hold values from -6 to 6
- dir_field: bfloat16 [64, 6, 48, 512], P('tx', None, 'lz', 'ty'), may hold values from -6 to 6
- border_b: bfloat16 [64, 6, 48, 512], P('tx', None, 'lz', 'ty')
- border_c: bfloat16 [64, 6, 48, 512], P('tx', None, 'lz', 'ty')
- land_mask: int32 [64, 512], P('tx', 'ty'), may hold values from 0 to 1, as said below
- active_rows: int32 [64, 4], P('tx', 'ty'), may hold values from -1 to 31, as said below
- cell_blocks: bfloat16 [64, 36, 512], P('tx', None, 'ty'), may hold values from -2.5 to 2.5
- column_k: bfloat16 [288, 288], replicated, may hold values from -0.375 to 0.375
- kappa: float32 [6], replicated, may hold values from 0.2 to 1
Outputs:
- test_image: bfloat16 [64, 6, 48, 512], P('tx', None, 'lz', 'ty')
- dir_image: bfloat16 [64, 6, 48, 512], P('tx', None, 'lz', 'ty')
- border: float32 [3], replicated
Inputs may be any that keep to these rules, and one draw needn't show every extreme that they name: `active_rows`: in each tile the 32 entries name distinct local rows, the active ones, followed by -1 for the rest; some tile has all 32 rows active. `land_mask`: cells whose latitude index y has y % 128 equal to 0 or 127 are ocean.
All inputs are finite; a program needn't handle non-finite values.
Results may differ from a plain program's by a relative error of at most 0.0028.
Values may be sent and summed in bfloat16 or wider, within the bound.
A program may use at most 192 MiB of HBM per device.

v0:
```python
import jax
import jax.numpy as jnp
from jax import lax
from jax.sharding import PartitionSpec as P


def extended(value, sides, width, wrap):
    for axis, dim in sides:
        size, length = (lax.axis_size(axis), value.shape[dim])
        up = [(i, (i + 1) % size) for i in range(size if wrap else size - 1)]
        down = [(j, i) for i, j in up]
        last = lax.slice_in_dim(value, length - width, length, axis=dim)
        initial = lax.slice_in_dim(value, 0, width, axis=dim)
        before = lax.ppermute(last, axis, up)
        after = lax.ppermute(initial, axis, down)
        value = jnp.concatenate([before, value, after], axis=dim)
    return value


def body(
    test_field, dir_field, border_b, border_c, land_mask, active_rows, cell_blocks, column_k, kappa
):
    rows_here, units, layers, cells = test_field.shape
    col_size = column_k.shape[0]
    depth = col_size // units
    lines = jnp.arange(rows_here, dtype=jnp.int32)
    named = jnp.any(active_rows[:, 0][None, :] == lines[:, None], axis=1)
    weight = land_mask.astype(jnp.float32) * named.astype(jnp.float32)[:, None]
    stacked = jnp.concatenate(
        [
            test_field * weight.astype(jnp.bfloat16)[:, None, None, :],
            dir_field * weight.astype(jnp.bfloat16)[:, None, None, :],
        ],
        axis=1,
    )
    column_b = border_b.astype(jnp.float32)
    row_c = border_c.astype(jnp.float32)
    norm_b = jnp.sum(column_b * column_b)
    norm_c = jnp.sum(row_c * row_c)
    value_c = jnp.sum(row_c * test_field.astype(jnp.float32))
    part = lax.all_to_all(stacked, "lz", split_axis=0, concat_axis=2, tiled=True)
    group = part.shape[0]
    span = part.shape[3]
    flat = part.reshape(group, 2, col_size, span)
    product = jnp.einsum("pq,gfqc->gfpc", column_k, flat, preferred_element_type=jnp.float32)
    product = product.astype(jnp.bfloat16).reshape(group, 2 * units, depth, span)
    coupled = lax.all_to_all(product, "lz", split_axis=2, concat_axis=0, tiled=True).astype(
        jnp.float32
    )
    lon_padded = extended(stacked, (("tx", 0),), 1, True)
    lat_padded = extended(stacked, (("ty", 3),), 1, False)
    center = stacked.astype(jnp.float32)
    spread = (
        lon_padded[2:].astype(jnp.float32)
        + lon_padded[:-2].astype(jnp.float32)
        + lat_padded[..., 2:].astype(jnp.float32)
        + lat_padded[..., :-2].astype(jnp.float32)
        - 4.0 * center
    )
    rates = jnp.concatenate([kappa, kappa]).reshape(1, 2 * units, 1, 1)
    blocks = cell_blocks.reshape(rows_here, units, units, cells)
    local = jnp.einsum(
        "xuwy,xfwzy->xfuzy",
        blocks,
        stacked.reshape(rows_here, 2, units, layers, cells),
        preferred_element_type=jnp.float32,
    ).reshape(rows_here, 2 * units, layers, cells)
    image = weight[:, None, None, :] * (coupled + local + rates * spread)
    test_full = image[:, :units]
    dir_full = image[:, units:]
    value_a = jnp.sum(column_b * test_full)
    value_e = jnp.sum(column_b * dir_full)
    norm_b, norm_c, value_c, value_a, value_e = lax.psum(
        (norm_b, norm_c, value_c, value_a, value_e), ("tx", "ty", "lz")
    )
    border = jnp.stack(
        [value_a / jnp.sqrt(norm_b), value_e / jnp.sqrt(norm_b), value_c / jnp.sqrt(norm_c)]
    )
    return (test_full.astype(jnp.bfloat16), dir_full.astype(jnp.bfloat16), border)


def solution(mesh):
    in_specs = (
        P("tx", None, "lz", "ty"),
        P("tx", None, "lz", "ty"),
        P("tx", None, "lz", "ty"),
        P("tx", None, "lz", "ty"),
        P("tx", "ty"),
        P("tx", "ty"),
        P("tx", None, "ty"),
        P(),
        P(),
    )
    out_specs = (P("tx", None, "lz", "ty"), P("tx", None, "lz", "ty"), P())
    return jax.shard_map(body, mesh=mesh, in_specs=in_specs, out_specs=out_specs, check_vma=False)
```

profile of v0, /device:TPU:0, one launch (start us, length us, event | category | flops | bytes accessed | tf_op | source)
XLA Modules:
  0.0 150.9 jit_solution(9420423562500274029)
XLA Ops:
  0.6 0.8 fusion.13
  1.5 0.8 fusion.14
  2.3 1.3 broadcast_multiply_fusion.1
  3.6 0.1 pad_maximum_fusion
  3.7 1.7 %copy.43 = bf16[32,12,12,128]{3,2,1,0:T(8,128)(2,1)} copy(bf16[32,12,12,128]{3,0,2,1:T(8,128)(2,1)S(1)} %pad_maximum_fusion) | data formatting | bytes 2359296 | tf_op jit(solution)/shard_map/concatenate | solution.py:29
  5.4 6.3 %all-to-all-start = ((bf16[32,12,12,128]{3,2,1,0:T(8,128)(2,1)}), bf16[32,12,12,128]{3,2,1,0:T(8,128)(2,1)}, u32[]{:S(2)}, u32[]{:S(2)}) async-start(bf16[32,12,12,128]{3,2,1,0:T(8,128)(2,1)} %copy.43), calls=%async_computation | async-start | bytes 3145728 | tf_op jit(solution)/shard_map/all_to_all | solution.py:41
  11.7 1.9 %fusion.7 = (bf16[32,12,12,1]{3,0,2,1:T(8,128)(2,1)}, bf16[32,12,12,1]{3,0,2,1:T(8,128)(2,1)}) fusion(bf16[32,6,12,128]{3,0,2,1:T(8,128)(2,1)S(1)} %get-tuple-element.21, bf16[32,6,12,128]{3,0,2,1:T(8,128)(2,1)S(1)} %get-tuple-element.22), kind=kLoop, calls=%fused_computation.25 | loop fusion | flops 9216 | bytes 1198080 | tf_op jit(solution)/shard_map/concatenate | solution.py:29
  13.6 2.4 %copy.53 = bf16[32,12,12,1]{0,2,3,1:T(8,128)(2,1)S(1)} copy(bf16[32,12,12,1]{3,0,2,1:T(8,128)(2,1)} %get-tuple-element.19) | data formatting | bytes 18432 | tf_op jit(solution)/shard_map/slice | solution.py:13
  16.0 1.3 collective-permute-start.2
  17.3 2.5 %copy.55 = bf16[32,12,12,1]{0,2,3,1:T(8,128)(2,1)S(1)} copy(bf16[32,12,12,1]{3,0,2,1:T(8,128)(2,1)} %get-tuple-element.20) | data formatting | bytes 18432 | tf_op jit(solution)/shard_map/slice | solution.py:12
  19.8 4.6 %collective-permute-start.3 = (bf16[32,12,12,1]{0,2,3,1:T(8,128)(2,1)S(1)}, bf16[32,12,12,1]{0,2,3,1:T(8,128)(2,1)S(1)}, u32[]{:S(2)}, u32[]{:S(2)}) collective-permute-start(bf16[32,12,12,1]{0,2,3,1:T(8,128)(2,1)S(1)} %copy.55), channel_id=1, source_target_pairs={{0,4},{4,8},{8,12},{1,5},{5,9},{9,13},{2,6},{6,10},{10,14},{3,7},{... | collective-permute-start | bytes 27656 | tf_op jit(solution)/shard_map/ppermute | solution.py:14
  24.4 0.2 fusion.11
  24.6 0.5 collective-permute-start.1
  25.1 10.2 %copy.50 = bf16[32,2,6,12,128]{3,2,1,4,0:T(8,128)(2,1)} copy(bf16[32,2,6,12,128]{4,0,3,2,1:T(8,128)(2,1)S(1)} %bitcast.37) | data formatting | bytes 2359296 | tf_op jit(solution)/shard_map/reshape | solution.py:65
  35.3 5.5 %copy.58 = bf16[32,6,6,128,1]{2,1,4,3,0:T(8,128)(2,1)} copy(bf16[32,6,6,128,1]{3,0,2,1,4:T(8,128)(2,1)S(1)} %bitcast.41) | data formatting | bytes 589824 | tf_op jit(solution)/shard_map/reshape | solution.py:61
  40.8 1.0 fusion.3
  41.8 7.0 %all-to-all-done = bf16[32,12,12,128]{3,2,1,0:T(8,128)(2,1)} async-done(((bf16[32,12,12,128]{3,2,1,0:T(8,128)(2,1)}), bf16[32,12,12,128]{3,2,1,0:T(8,128)(2,1)}, u32[]{:S(2)}, u32[]{:S(2)}) %all-to-all-start) | async-done | bytes 1179680 | tf_op jit(solution)/shard_map/all_to_all | solution.py:41
  48.8 2.8 %copy.45 = bf16[8,12,4,12,128]{4,0,3,2,1:T(8,128)(2,1)S(1)} copy(bf16[8,12,4,12,128]{4,3,1,0,2:T(8,128)(2,1)} %bitcast.3) | data formatting | bytes 2359296 | tf_op jit(solution)/shard_map/all_to_all | solution.py:41
  51.6 0.8 convolution_convert_fusion
  52.4 1.9 %copy.47 = bf16[8,12,48,128]{3,0,1,2:T(8,128)(2,1)} copy(bf16[8,12,48,128]{3,2,1,0:T(8,128)(2,1)S(1)} %bitcast.39) | data formatting | bytes 2359296 | tf_op jit(solution)/shard_map/reshape | solution.py:46
  54.2 4.5 %all-to-all-start.1 = ((bf16[8,12,48,128]{3,0,1,2:T(8,128)(2,1)}), bf16[8,12,48,128]{3,0,1,2:T(8,128)(2,1)}, u32[]{:S(2)}, u32[]{:S(2)}) async-start(bf16[8,12,48,128]{3,0,1,2:T(8,128)(2,1)} %copy.47), calls=%async_computation.1 | async-start | bytes 2359296 | tf_op jit(solution)/shard_map/all_to_all | solution.py:47
  58.7 20.0 %convolution_bitcast_fusion = f32[32,2,6,12,128]{3,2,1,4,0:T(8,128)} fusion(bf16[32,2,6,12,128]{3,2,1,4,0:T(8,128)(2,1)} %copy.50, bf16[32,6,6,128,1]{2,1,4,3,0:T(8,128)(2,1)} %copy.58), kind=kOutput, calls=%fused_computation | convolution fusion | flops 7077888 | bytes 3833856 | tf_op jit(solution)/shard_map/xuwy,xfwzy->xfuzy/dot_general | solution.py:62
  78.7 0.1 pad_maximum_fusion.9
  78.8 15.6 %copy.52 = f32[32,2,6,12,128]{4,0,3,2,1:T(8,128)} copy(f32[32,2,6,12,128]{3,2,1,4,0:T(8,128)} %convolution_bitcast_fusion) | data formatting | bytes 4718592 | tf_op jit(solution)/shard_map/xuwy,xfwzy->xfuzy/transpose | solution.py:62
  94.4 1.0 copy.54
  95.4 1.9 %copy.56 = bf16[32,12,12,1]{3,0,2,1:T(8,128)(2,1)} copy(bf16[32,12,12,1]{0,2,3,1:T(8,128)(2,1)S(1)} %collective-permute-done.3) | data formatting | bytes 18432 | tf_op jit(solution)/shard_map/ppermute | solution.py:14
  97.3 1.6 %copy.48 = bf16[8,12,48,128]{3,0,2,1:T(8,128)(2,1)S(1)} copy(bf16[8,12,48,128]{3,0,1,2:T(8,128)(2,1)} %all-to-all-done.1) | data formatting | bytes 2359296 | tf_op jit(solution)/shard_map/all_to_all | solution.py:47
  99.0 4.8 %fusion.1 = f32[32,12,12,128]{3,0,2,1:T(8,128)S(1)} fusion(f32[32,2,6,12,128]{4,0,3,2,1:T(8,128)} %copy.52, bf16[32,12,12,1]{3,0,2,1:T(8,128)(2,1)S(1)} %copy-done.2, bf16[32,6,12,128]{3,0,2,1:T(8,128)(2,1)S(1)} %get-tuple-element.22, bf16[32,6,12,128]{3,0,2,1:T(8,128)(2,1)S(1)} %get-tuple-element.21, bf16[32,12,12,1]{3,0,2,1:T(8,128)(2,1)S(1)} %copy.54, ...), kind=kLoop, calls=%fused_computation.4 | loop fusion | flops 22413312 | bytes 7186480 | tf_op jit(solution)/shard_map/mul | solution.py:68
  103.8 1.3 fusion.15
  105.1 1.1 fusion.4
  106.2 40.9 %all-reduce = (f32[]{:T(128)}, f32[]{:T(128)}, f32[]{:T(128)}, f32[]{:T(128)}, f32[]{:T(128)}) all-reduce(f32[]{:T(128)} %get-tuple-element.7, f32[]{:T(128)} %get-tuple-element.6, f32[]{:T(128)} %get-tuple-element.4, f32[]{:T(128)} %get-tuple-element.5, f32[]{:T(128)} %get-tuple-element.3), channel_id=1, replica_groups=mesh['tx'=2,'ty'=4,'lz'=4] {'tx','ty','lz'}, use_global_device_ids=true, to_apply=%region_8.0 | all-reduce | flops 5 | bytes 40 | tf_op jit(solution)/shard_map/psum | solution.py:73
  150.3 0.6 pad_maximum_fusion.10
  (23 shorter events, 0.1 us)
Async XLA Ops:
  0.6 50.9 %copy-start = (bf16[288,288]{1,0:T(8,128)(2,1)S(1)}, bf16[288,288]{1,0:T(8,128)(2,1)}, u32[]{:S(2)}) copy-start(bf16[288,288]{1,0:T(8,128)(2,1)} %param.16) | copy-start | bytes 497668
  5.4 43.4 %all-to-all-start = ((bf16[32,12,12,128]{3,2,1,0:T(8,128)(2,1)}), bf16[32,12,12,128]{3,2,1,0:T(8,128)(2,1)}, u32[]{:S(2)}, u32[]{:S(2)}) async-start(bf16[32,12,12,128]{3,2,1,0:T(8,128)(2,1)} %copy.43), calls=%async_computation | async-start | bytes 3145728 | tf_op jit(solution)/shard_map/all_to_all | solution.py:41
  16.0 78.4 %collective-permute-start.2 = (bf16[32,12,12,1]{0,2,3,1:T(8,128)(2,1)S(1)}, bf16[32,12,12,1]{0,2,3,1:T(8,128)(2,1)S(1)}, u32[]{:S(2)}, u32[]{:S(2)}) collective-permute-start(bf16[32,12,12,1]{0,2,3,1:T(8,128)(2,1)S(1)} %copy.53), channel_id=1, source_target_pairs={{4,0},{8,4},{12,8},{5,1},{9,5},{13,9},{6,2},{10,6},{14,10},{7,3},{... | collective-permute-start | bytes 27656 | tf_op jit(solution)/shard_map/ppermute | solution.py:15
  19.8 75.6 %collective-permute-start.3 = (bf16[32,12,12,1]{0,2,3,1:T(8,128)(2,1)S(1)}, bf16[32,12,12,1]{0,2,3,1:T(8,128)(2,1)S(1)}, u32[]{:S(2)}, u32[]{:S(2)}) collective-permute-start(bf16[32,12,12,1]{0,2,3,1:T(8,128)(2,1)S(1)} %copy.55), channel_id=1, source_target_pairs={{0,4},{4,8},{8,12},{1,5},{5,9},{9,13},{2,6},{6,10},{10,14},{3,7},{... | collective-permute-start | bytes 27656 | tf_op jit(solution)/shard_map/ppermute | solution.py:14
  24.5 74.5 %collective-permute-start = (bf16[1,12,12,128]{3,0,2,1:T(2,128)(2,1)S(1)}, bf16[1,12,12,128]{3,0,2,1:T(2,128)(2,1)S(1)}, u32[]{:S(2)}, u32[]{:S(2)}) collective-permute-start(bf16[1,12,12,128]{3,0,2,1:T(2,128)(2,1)S(1)} %get-tuple-element.17), channel_id=1, source_target_pairs={{16,0},{0,16},{17,1},{1,17},{18,2},{2,18},{19,3},{3,19},{20,4},{4,... | collective-permute-start | bytes 110600 | tf_op jit(solution)/shard_map/ppermute | solution.py:15
  24.6 74.4 %collective-permute-start.1 = (bf16[1,12,12,128]{3,0,2,1:T(2,128)(2,1)S(1)}, bf16[1,12,12,128]{3,0,2,1:T(2,128)(2,1)S(1)}, u32[]{:S(2)}, u32[]{:S(2)}) collective-permute-start(bf16[1,12,12,128]{3,0,2,1:T(2,128)(2,1)S(1)} %get-tuple-element.18), channel_id=1, source_target_pairs={{0,16},{16,0},{1,17},{17,1},{2,18},{18,2},{3,19},{19,3},{4,20},{20... | collective-permute-start | bytes 110600 | tf_op jit(solution)/shard_map/ppermute | solution.py:14
  25.1 10.2 %copy-start.6 = (bf16[32,36,128]{2,0,1:T(8,128)(2,1)S(1)}, bf16[32,36,128]{2,0,1:T(8,128)(2,1)}, u32[]{:S(2)}) copy-start(bf16[32,36,128]{2,0,1:T(8,128)(2,1)} %param.15) | copy-start | bytes 884740
  35.3 5.5 %copy-start.3 = (bf16[32,6,12,128]{3,0,2,1:T(8,128)(2,1)S(1)}, bf16[32,6,12,128]{3,0,2,1:T(8,128)(2,1)}, u32[]{:S(2)}) copy-start(bf16[32,6,12,128]{3,0,2,1:T(8,128)(2,1)} %param.9) | copy-start | bytes 1769476
  35.3 5.5 %copy-start.4 = (bf16[32,6,12,128]{3,0,2,1:T(8,128)(2,1)S(1)}, bf16[32,6,12,128]{3,0,2,1:T(8,128)(2,1)}, u32[]{:S(2)}) copy-start(bf16[32,6,12,128]{3,0,2,1:T(8,128)(2,1)} %param.12) | copy-start | bytes 1769476
  54.2 43.1 %all-to-all-start.1 = ((bf16[8,12,48,128]{3,0,1,2:T(8,128)(2,1)}), bf16[8,12,48,128]{3,0,1,2:T(8,128)(2,1)}, u32[]{:S(2)}, u32[]{:S(2)}) async-start(bf16[8,12,48,128]{3,0,1,2:T(8,128)(2,1)} %copy.47), calls=%async_computation.1 | async-start | bytes 2359296 | tf_op jit(solution)/shard_map/all_to_all | solution.py:47
  58.7 20.0 %copy-start.7 = (f32[6]{0:T(128)S(1)}, f32[6]{0:T(128)}, u32[]{:S(2)}) copy-start(f32[6]{0:T(128)} %param.17) | copy-start | bytes 76
  97.3 1.7 %copy-start.2 = (bf16[32,12,12,1]{3,0,2,1:T(8,128)(2,1)S(1)}, bf16[32,12,12,1]{3,0,2,1:T(8,128)(2,1)}, u32[]{:S(2)}) copy-start(bf16[32,12,12,1]{3,0,2,1:T(8,128)(2,1)} %copy.56) | copy-start | bytes 27652
  103.8 1.3 copy-start.5
  103.8 47.1 %copy-start.1 = (bf16[288,288]{1,0:T(8,128)(2,1)S(1)}, bf16[288,288]{1,0:T(8,128)(2,1)}, u32[]{:S(2)}) copy-start(bf16[288,288]{1,0:T(8,128)(2,1)} %param.16) | copy-start | bytes 497668
where the time goes:
time: 152 us; the launch traced here: 151 us
  local copies, waits for them, and re-layouts  48.4 us (32%)
  blocking collectives  40.9 us (27%)
  matrix products  20.8 us (14%)
  starting transfers between devices  17.2 us (11%)
  other arithmetic  12.6 us (8%)
  waiting for transfers between devices  7.02 us (5%)
  between operations  3.94 us (3%)
    psum x1, blocking collectives, body(): lax.psum((norm_b, norm_c, value_c, value_a, value_e), ('tx', 'ty', 'lz'))  40.9 us
    dot_general x1, matrix products, body(): jnp.einsum('xuwy,xfwzy->xfuzy', blocks, stacked.reshape(rows_here, 2, uni...  20 us
    transpose x1, local copies, waits for them, and re-layouts, body(): jnp.einsum('xuwy,xfwzy->xfuzy', blocks, stacked.reshape(rows_here, 2, uni...  15.6 us
    reshape x1, local copies, waits for them, and re-layouts, body(): stacked.reshape(rows_here, 2, units, layers, cells)  10.2 us
    all_to_all x1, waiting for transfers between devices, body(): lax.all_to_all(stacked, 'lz', split_axis=0, concat_axis=2, tiled=True)  7.01 us
    all_to_all x1, starting transfers between devices, body(): lax.all_to_all(stacked, 'lz', split_axis=0, concat_axis=2, tiled=True)  6.35 us
    reshape x1, local copies, waits for them, and re-layouts, body(): blocks = cell_blocks.reshape(rows_here, units, units, cells)  5.47 us
    ppermute x2, starting transfers between devices, extended(): before = lax.ppermute(last, axis, up)  5.05 us
  transfers between devices with their start and end apart: 6, of which 1 were waited for; matrix products, arithmetic and copies ran while one was open for 46% of the time, Pallas kernels for 0%

commit v1 on v0

--- a/solution.py
+++ b/solution.py
@@ -38,7 +38,10 @@
     norm_b = jnp.sum(column_b * column_b)
     norm_c = jnp.sum(row_c * row_c)
     value_c = jnp.sum(row_c * test_field.astype(jnp.float32))
-    part = lax.all_to_all(stacked, "lz", split_axis=0, concat_axis=2, tiled=True)
+    n_dev = lax.axis_size("lz")
+    pieces = jnp.stack(jnp.split(stacked, n_dev, axis=0), axis=0)
+    pieces = lax.all_to_all(pieces, "lz", split_axis=0, concat_axis=0)
+    part = jnp.concatenate(pieces, axis=2)
     group = part.shape[0]
     span = part.shape[3]
     flat = part.reshape(group, 2, col_size, span)

time: 152 us -> 142 us (0.934)
  waiting for transfers between devices: 7.02 us -> 1.34 us
  local copies, waits for them, and re-layouts: 48.4 us -> 44.4 us
    all_to_all x1, waiting for transfers between devices: 7.01 us -> 1.33 us  [body(): pieces = lax.all_to_all(pieces, 'lz', split_axis=0, concat_axis=0)]
    concatenate x1 -> x0, local copies, waits for them, and re-layouts: 1.67 us -> none  [body(): jnp.concatenate([test_field * weight.astype(jnp.bfloat16)[:, None, None,...]
    ppermute x2, starting transfers between devices: 5.05 us -> 3.47 us  [extended(): before = lax.ppermute(last, axis, up)]
  transfers between devices with their start and end apart: 6 -> 6, of which waited for: 1 -> 1; matrix products, arithmetic and copies ran while one was open for 46% -> 47% of each run, Pallas kernels for 0% -> 0%
where the time goes in v1:
time: 142 us
  local copies, waits for them, and re-layouts  44.4 us (31%)
  blocking collectives  41.6 us (29%)
  matrix products  20.8 us (15%)
  starting transfers between devices  16.1 us (11%)
  other arithmetic  13.3 us (9%)
  between operations  4.04 us (3%)
    psum x1, blocking collectives, body(): lax.psum((norm_b, norm_c, value_c, value_a, value_e), ('tx', 'ty', 'lz'))  41.6 us
    dot_general x1, matrix products, body(): jnp.einsum('xuwy,xfwzy->xfuzy', blocks, stacked.reshape(rows_here, 2, uni...  20 us
    transpose x1, local copies, waits for them, and re-layouts, body(): jnp.einsum('xuwy,xfwzy->xfuzy', blocks, stacked.reshape(rows_here, 2, uni...  15.7 us
    reshape x1, local copies, waits for them, and re-layouts, body(): stacked.reshape(rows_here, 2, units, layers, cells)  10.2 us
    all_to_all x1, starting transfers between devices, body(): pieces = lax.all_to_all(pieces, 'lz', split_axis=0, concat_axis=0)  6.35 us
    reshape x1, local copies, waits for them, and re-layouts, body(): blocks = cell_blocks.reshape(rows_here, units, units, cells)  5.48 us
    mul x1, other arithmetic, body(): image = weight[:, None, None, :] * (coupled + local + rates * spread)  4.71 us
    all_to_all x1, starting transfers between devices, body(): lax.all_to_all(product, 'lz', split_axis=2, concat_axis=0, tiled=True)  4.47 us
  transfers between devices with their start and end apart: 6, of which 1 were waited for; matrix products, arithmetic and copies ran while one was open for 47% of the time, Pallas kernels for 0%

profile of v1, /device:TPU:0, one launch (start us, length us, event | category | flops | bytes accessed | tf_op | source)
XLA Modules:
  0.0 141.6 jit_solution(2436970044934268014)
XLA Ops:
  0.6 0.8 fusion.21
  1.5 0.8 fusion.22
  2.3 1.3 broadcast_multiply_fusion.1
  3.6 0.1 fusion.11
  3.7 1.2 pad_maximum_fusion.9
  4.9 6.3 %all-to-all-start = ((bf16[4,8,12,12,128]{4,1,3,2,0:T(8,128)(2,1)}), bf16[4,8,12,12,128]{4,1,3,2,0:T(8,128)(2,1)}, u32[]{:S(2)}, u32[]{:S(2)}) async-start(bf16[4,8,12,12,128]{4,1,3,2,0:T(8,128)(2,1)} %pad_maximum_fusion.9), calls=%async_computation | async-start | bytes 2359296 | tf_op jit(solution)/shard_map/all_to_all | solution.py:43
  11.3 1.5 %fusion.7 = (bf16[32,12,12,1]{3,0,2,1:T(8,128)(2,1)S(1)}, bf16[32,12,12,1]{3,0,2,1:T(8,128)(2,1)}) fusion(bf16[32,6,12,128]{3,0,2,1:T(8,128)(2,1)S(1)} %get-tuple-element.25, bf16[32,6,12,128]{3,0,2,1:T(8,128)(2,1)S(1)} %get-tuple-element.26), kind=kLoop, calls=%fused_computation.33 | loop fusion | flops 9216 | bytes 1198080 | tf_op jit(solution)/shard_map/concatenate | solution.py:29
  12.7 2.4 %copy.59 = bf16[32,12,12,1]{0,2,3,1:T(8,128)(2,1)S(1)} copy(bf16[32,12,12,1]{3,0,2,1:T(8,128)(2,1)} %get-tuple-element.20) | data formatting | bytes 18432 | tf_op jit(solution)/shard_map/slice | solution.py:12
  15.2 3.4 %collective-permute-start.3 = (bf16[32,12,12,1]{0,2,3,1:T(8,128)(2,1)S(1)}, bf16[32,12,12,1]{0,2,3,1:T(8,128)(2,1)S(1)}, u32[]{:S(2)}, u32[]{:S(2)}) collective-permute-start(bf16[32,12,12,1]{0,2,3,1:T(8,128)(2,1)S(1)} %copy.59), channel_id=1, source_target_pairs={{0,4},{4,8},{8,12},{1,5},{5,9},{9,13},{2,6},{6,10},{10,14},{3,7},{... | collective-permute-start | bytes 27656 | tf_op jit(solution)/shard_map/ppermute | solution.py:14
  18.6 1.2 copy.57
  19.8 1.3 collective-permute-start.2
  21.1 0.2 fusion.19
  21.4 0.5 collective-permute-start
  22.0 10.2 %copy.54 = bf16[32,2,6,12,128]{3,2,1,4,0:T(8,128)(2,1)} copy(bf16[32,2,6,12,128]{4,0,3,2,1:T(8,128)(2,1)S(1)} %bitcast.45) | data formatting | bytes 2359296 | tf_op jit(solution)/shard_map/reshape | solution.py:68
  32.2 5.5 %copy.62 = bf16[32,6,6,128,1]{2,1,4,3,0:T(8,128)(2,1)} copy(bf16[32,6,6,128,1]{3,0,2,1,4:T(8,128)(2,1)S(1)} %bitcast.48) | data formatting | bytes 589824 | tf_op jit(solution)/shard_map/reshape | solution.py:64
  37.7 0.9 fusion.3
  38.6 1.3 all-to-all-done
  39.9 1.4 copy.49
  41.3 0.8 convolution_convert_fusion
  42.1 1.9 %copy.51 = bf16[8,12,48,128]{3,0,1,2:T(8,128)(2,1)} copy(bf16[8,12,48,128]{3,2,1,0:T(8,128)(2,1)S(1)} %bitcast.47) | data formatting | bytes 2359296 | tf_op jit(solution)/shard_map/reshape | solution.py:49
  43.9 4.5 %all-to-all-start.1 = ((bf16[8,12,48,128]{3,0,1,2:T(8,128)(2,1)}), bf16[8,12,48,128]{3,0,1,2:T(8,128)(2,1)}, u32[]{:S(2)}, u32[]{:S(2)}) async-start(bf16[8,12,48,128]{3,0,1,2:T(8,128)(2,1)} %copy.51), calls=%async_computation.1 | async-start | bytes 2359296 | tf_op jit(solution)/shard_map/all_to_all | solution.py:50
  48.4 20.0 %convolution_bitcast_fusion = f32[32,2,6,12,128]{3,2,1,4,0:T(8,128)} fusion(bf16[32,2,6,12,128]{3,2,1,4,0:T(8,128)(2,1)} %copy.54, bf16[32,6,6,128,1]{2,1,4,3,0:T(8,128)(2,1)} %copy.62), kind=kOutput, calls=%fused_computation | convolution fusion | flops 7077888 | bytes 3833856 | tf_op jit(solution)/shard_map/xuwy,xfwzy->xfuzy/dot_general | solution.py:65
  68.5 15.7 %copy.56 = f32[32,2,6,12,128]{4,0,3,2,1:T(8,128)} copy(f32[32,2,6,12,128]{3,2,1,4,0:T(8,128)} %convolution_bitcast_fusion) | data formatting | bytes 4718592 | tf_op jit(solution)/shard_map/xuwy,xfwzy->xfuzy/transpose | solution.py:65
  84.1 1.0 copy.60
  85.1 1.9 %copy.58 = bf16[32,12,12,1]{3,0,2,1:T(8,128)(2,1)} copy(bf16[32,12,12,1]{0,2,3,1:T(8,128)(2,1)S(1)} %collective-permute-done.2) | data formatting | bytes 18432 | tf_op jit(solution)/shard_map/ppermute | solution.py:15
  87.1 1.7 %copy.52 = bf16[8,12,48,128]{3,0,2,1:T(8,128)(2,1)S(1)} copy(bf16[8,12,48,128]{3,0,1,2:T(8,128)(2,1)} %all-to-all-done.1) | data formatting | bytes 2359296 | tf_op jit(solution)/shard_map/all_to_all | solution.py:50
  88.8 0.3 copy-done.2
  89.1 4.7 %fusion.1 = f32[32,12,12,128]{3,0,2,1:T(8,128)S(1)} fusion(f32[32,2,6,12,128]{4,0,3,2,1:T(8,128)S(1)} %copy-done.2, bf16[32,12,12,1]{3,0,2,1:T(8,128)(2,1)S(1)} %copy.60, bf16[32,6,12,128]{3,0,2,1:T(8,128)(2,1)S(1)} %get-tuple-element.26, bf16[32,6,12,128]{3,0,2,1:T(8,128)(2,1)S(1)} %get-tuple-element.25, bf16[32,12,12,1]{3,0,2,1:T(8,128)(2,1)} %copy.58, ...), kind=kLoop, calls=%fused_computation.21 | loop fusion | flops 22413312 | bytes 7186480 | tf_op jit(solution)/shard_map/mul | solution.py:71
  93.8 1.3 fusion.23
  95.1 1.1 fusion.4
  96.2 41.6 %all-reduce = (f32[]{:T(128)}, f32[]{:T(128)}, f32[]{:T(128)}, f32[]{:T(128)}, f32[]{:T(128)}) all-reduce(f32[]{:T(128)} %get-tuple-element.7, f32[]{:T(128)} %get-tuple-element.6, f32[]{:T(128)} %get-tuple-element.4, f32[]{:T(128)} %get-tuple-element.5, f32[]{:T(128)} %get-tuple-element.3), channel_id=1, replica_groups=mesh['tx'=2,'ty'=4,'lz'=4] {'tx','ty','lz'}, use_global_device_ids=true, to_apply=%region_8.0 | all-reduce | flops 5 | bytes 40 | tf_op jit(solution)/shard_map/psum | solution.py:76
  141.0 0.6 pad_maximum_fusion.11
  (24 shorter events, 0.3 us)
Async XLA Ops:
  0.6 40.7 %copy-start = (bf16[288,288]{1,0:T(8,128)(2,1)S(1)}, bf16[288,288]{1,0:T(8,128)(2,1)}, u32[]{:S(2)}) copy-start(bf16[288,288]{1,0:T(8,128)(2,1)} %param.16) | copy-start | bytes 497668
  4.9 35.0 %all-to-all-start = ((bf16[4,8,12,12,128]{4,1,3,2,0:T(8,128)(2,1)}), bf16[4,8,12,12,128]{4,1,3,2,0:T(8,128)(2,1)}, u32[]{:S(2)}, u32[]{:S(2)}) async-start(bf16[4,8,12,12,128]{4,1,3,2,0:T(8,128)(2,1)} %pad_maximum_fusion.9), calls=%async_computation | async-start | bytes 2359296 | tf_op jit(solution)/shard_map/all_to_all | solution.py:43
  15.2 69.0 %collective-permute-start.3 = (bf16[32,12,12,1]{0,2,3,1:T(8,128)(2,1)S(1)}, bf16[32,12,12,1]{0,2,3,1:T(8,128)(2,1)S(1)}, u32[]{:S(2)}, u32[]{:S(2)}) collective-permute-start(bf16[32,12,12,1]{0,2,3,1:T(8,128)(2,1)S(1)} %copy.59), channel_id=1, source_target_pairs={{0,4},{4,8},{8,12},{1,5},{5,9},{9,13},{2,6},{6,10},{10,14},{3,7},{... | collective-permute-start | bytes 27656 | tf_op jit(solution)/shard_map/ppermute | solution.py:14
  19.8 65.3 %collective-permute-start.2 = (bf16[32,12,12,1]{0,2,3,1:T(8,128)(2,1)S(1)}, bf16[32,12,12,1]{0,2,3,1:T(8,128)(2,1)S(1)}, u32[]{:S(2)}, u32[]{:S(2)}) collective-permute-start(bf16[32,12,12,1]{0,2,3,1:T(8,128)(2,1)S(1)} %copy.57), channel_id=1, source_target_pairs={{4,0},{8,4},{12,8},{5,1},{9,5},{13,9},{6,2},{10,6},{14,10},{7,3},{... | collective-permute-start | bytes 27656 | tf_op jit(solution)/shard_map/ppermute | solution.py:15
  21.3 67.5 %collective-permute-start.1 = (bf16[1,12,12,128]{3,0,2,1:T(2,128)(2,1)S(1)}, bf16[1,12,12,128]{3,0,2,1:T(2,128)(2,1)S(1)}, u32[]{:S(2)}, u32[]{:S(2)}) collective-permute-start(bf16[1,12,12,128]{3,0,2,1:T(2,128)(2,1)S(1)} %get-tuple-element.18), channel_id=1, source_target_pairs={{0,16},{16,0},{1,17},{17,1},{2,18},{18,2},{3,19},{19,3},{4,20},{20... | collective-permute-start | bytes 110600 | tf_op jit(solution)/shard_map/ppermute | solution.py:14
  21.4 67.4 %collective-permute-start = (bf16[1,12,12,128]{3,0,2,1:T(2,128)(2,1)S(1)}, bf16[1,12,12,128]{3,0,2,1:T(2,128)(2,1)S(1)}, u32[]{:S(2)}, u32[]{:S(2)}) collective-permute-start(bf16[1,12,12,128]{3,0,2,1:T(2,128)(2,1)S(1)} %get-tuple-element.17), channel_id=1, source_target_pairs={{16,0},{0,16},{17,1},{1,17},{18,2},{2,18},{19,3},{3,19},{20,4},{4,... | collective-permute-start | bytes 110600 | tf_op jit(solution)/shard_map/ppermute | solution.py:15
  22.0 10.2 %copy-start.6 = (bf16[32,36,128]{2,0,1:T(8,128)(2,1)S(1)}, bf16[32,36,128]{2,0,1:T(8,128)(2,1)}, u32[]{:S(2)}) copy-start(bf16[32,36,128]{2,0,1:T(8,128)(2,1)} %param.15) | copy-start | bytes 884740
  32.2 5.5 %copy-start.3 = (bf16[32,6,12,128]{3,0,2,1:T(8,128)(2,1)S(1)}, bf16[32,6,12,128]{3,0,2,1:T(8,128)(2,1)}, u32[]{:S(2)}) copy-start(bf16[32,6,12,128]{3,0,2,1:T(8,128)(2,1)} %param.9) | copy-start | bytes 1769476
  32.2 5.5 %copy-start.4 = (bf16[32,6,12,128]{3,0,2,1:T(8,128)(2,1)S(1)}, bf16[32,6,12,128]{3,0,2,1:T(8,128)(2,1)}, u32[]{:S(2)}) copy-start(bf16[32,6,12,128]{3,0,2,1:T(8,128)(2,1)} %param.12) | copy-start | bytes 1769476
  43.9 43.1 %all-to-all-start.1 = ((bf16[8,12,48,128]{3,0,1,2:T(8,128)(2,1)}), bf16[8,12,48,128]{3,0,1,2:T(8,128)(2,1)}, u32[]{:S(2)}, u32[]{:S(2)}) async-start(bf16[8,12,48,128]{3,0,1,2:T(8,128)(2,1)} %copy.51), calls=%async_computation.1 | async-start | bytes 2359296 | tf_op jit(solution)/shard_map/all_to_all | solution.py:50
  48.4 20.0 %copy-start.7 = (f32[6]{0:T(128)S(1)}, f32[6]{0:T(128)}, u32[]{:S(2)}) copy-start(f32[6]{0:T(128)} %param.17) | copy-start | bytes 76
  87.1 2.0 %copy-start.2 = (f32[32,2,6,12,128]{4,0,3,2,1:T(8,128)S(1)}, f32[32,2,6,12,128]{4,0,3,2,1:T(8,128)}, u32[]{:S(2)}) copy-start(f32[32,2,6,12,128]{4,0,3,2,1:T(8,128)} %copy.56) | copy-start | bytes 7077892
  93.8 1.3 copy-start.5
  93.8 47.8 %copy-start.1 = (bf16[288,288]{1,0:T(8,128)(2,1)S(1)}, bf16[288,288]{1,0:T(8,128)(2,1)}, u32[]{:S(2)}) copy-start(bf16[288,288]{1,0:T(8,128)(2,1)} %param.16) | copy-start | bytes 497668
